TPU v7x, 256 devices: a whole 4x4x8 slice. The times are simulated.
256 devices in a mesh: group: 8 (over y, core), leaf: 32 (over z, x).
Axes of the slice: x: 4, y: 4, z: 8, core: 2. Of those that a mesh axis runs over, the one named last changes fastest.
Arguments:
- points: float32 [3, 524288], P(None, ('group', 'leaf')), may hold values from 0 to 1
- rhs: float32 [16, 524288], P(None, ('group', 'leaf')), may hold values from -0.5 to 0.5
- counts: int32 [4096], P(('group', 'leaf')), may hold values from 32 to 128
- basis: float32 [4096, 128, 32], P(('group', 'leaf')), may hold values from -1 to 1
- leaf_geom: float32 [4096, 4], P(('group', 'leaf')), may hold values from 0.05 to 1
- leaf_partners: int32 [4096, 16], P(('group', 'leaf')), may hold values from -16 to 16, as said below
- leaf_middle_owner: int32 [256, 16], P(('group', 'leaf')), may hold values from 0 to 7, never falling along the last dimension, each value on 1 to 4 neighbouring positions
- leaf_basis_transfer: float32 [4096, 32, 32], P(('group', 'leaf')), may hold values from -1 to 1
- mid_geom: float32 [2048, 4], P(('group', 'leaf')), may hold values from 0.05 to 1
- mid_parent: int32 [8, 256], P('group', 'leaf'), may hold values from 0 to 15, never falling along the last dimension, each value on 1 to 32 neighbouring positions
- mid_transfer: float32 [2048, 32, 32], P(('group', 'leaf')), may hold values from -1 to 1
- mid_peers: int32 [2048, 8], P(('group', 'leaf')), may hold values from 0 to 31, all different within a row; in each aligned block of 8 rows (0 to 7, 8 to 15, ...) at most 4 rows name the same one
- mid_slots: int32 [2048, 8], P(('group', 'leaf')), may hold values from 0 to 7
- top_geom: float32 [128, 4], P('group'), may hold values from 0.05 to 1
- top_offsets: int32 [128, 16], P('group'), may hold values from 1 to 127
Outputs:
- product: float32 [16, 524288], P(None, ('group', 'leaf'))
Inputs may be any that keep to these rules, and one draw needn't show every extreme that they name: `leaf_partners`: column 0 is 0. Every partner leaf lies in the same group, at most 16 leaves away. `mid_peers`: over the rows of one device, no device is named more than 4 times, and some device is named exactly 4 times; the names in a row differ. `leaf_middle_owner`: never falling along a row. `mid_parent`: never falling along a row.
All inputs are finite; a program needn't handle non-finite values.
Results may differ from a plain program's by a relative error of at most 0.00013.
Values sent between devices are 32-bit elements; how exact they have to be, the bound alone decides.
A program may use at most 64 MiB of HBM per device.

v0:
```python
import jax
import jax.numpy as jnp
from jax import lax
from jax.sharding import PartitionSpec as P

PTS = 128
RANK = 32
RHS = 16
TOP = 16
NEAR = 8
REACH = 16
exact_product = lax.Precision.HIGHEST
root_three = 1.7320508075688772
length_scale = 0.5


def extended(block, sides, width):
    for axis, dim in sides:
        count = lax.axis_size(axis)
        forward = [(i, i + 1) for i in range(count - 1)]
        backward = [(target, source) for source, target in forward]
        low = lax.ppermute(
            lax.slice_in_dim(block, block.shape[dim] - width, None, axis=dim), axis, forward
        )
        high = lax.ppermute(lax.slice_in_dim(block, 0, width, axis=dim), axis, backward)
        block = jnp.concatenate([low, block, high], axis=dim)
    return block


def node_table():
    indices = jnp.arange(RANK, dtype=jnp.int32)
    layers = []
    for axis_number in range(3):
        spread = (indices * (2 * axis_number + 3) % RANK).astype(jnp.float32)
        layers.append(jnp.cos(jnp.pi * (spread + 0.5) / RANK))
    return jnp.stack(layers)


def place_nodes(geometry, table):
    return geometry[..., :3, None] + geometry[..., 3:4, None] * table


def matern(left, right):
    squared = jnp.zeros((), jnp.float32)
    for axis_number in range(3):
        difference = left[..., axis_number, :, None] - right[..., axis_number, None, :]
        squared = squared + difference * difference
    distance = jnp.sqrt(squared)
    decay_rate = root_three / length_scale
    return (1.0 + decay_rate * distance) * jnp.exp(-decay_rate * distance)


def couple_rows(target_geom, source_point_rows, table):
    coeff_width = RANK * RHS
    target_nodes = place_nodes(target_geom, table)
    source_nodes = place_nodes(source_point_rows[..., coeff_width:], table)
    source_coeff = source_point_rows[..., :coeff_width].reshape(
        source_point_rows.shape[:-1] + (RANK, RHS)
    )
    coupling = matern(target_nodes[:, None], source_nodes)
    return jnp.einsum("njkm,njmr->nkr", coupling, source_coeff, precision=exact_product)


def on_device(
    points,
    rhs,
    counts,
    basis,
    leaf_geom,
    leaf_partners,
    leaf_middle_owner,
    leaf_basis_transfer,
    mid_geom,
    mid_parent,
    mid_transfer,
    mid_peers,
    mid_slots,
    top_geom,
    top_offsets,
):
    leaf_count = counts.shape[0]
    mid_count = mid_transfer.shape[0]
    coeff_width = RANK * RHS
    table = node_table()
    position = jnp.arange(PTS, dtype=jnp.int32)
    present = (position[None, :] < counts[:, None]).astype(jnp.float32)
    masked = rhs.reshape(RHS, leaf_count, PTS) * present[None]
    stacked = jnp.concatenate([masked.reshape(RHS, leaf_count * PTS), points], axis=0)
    padded = extended(stacked, (("leaf", 1),), REACH * PTS)
    grid = padded.reshape(RHS + 3, leaf_count + 2 * REACH, PTS)
    leaf_coefficient_rows = jnp.einsum("lpk,rlp->lkr", basis, masked, precision=exact_product)
    leaf_rows = jnp.concatenate(
        [leaf_coefficient_rows.reshape(leaf_count, coeff_width), leaf_geom], axis=1
    )
    leaf_padded = extended(leaf_rows, (("leaf", 0),), REACH)
    members = (
        leaf_middle_owner[0][None, :] == jnp.arange(mid_count, dtype=jnp.int32)[:, None]
    ).astype(jnp.float32)
    upward_coefficients = jnp.einsum(
        "qcz,qct->qzt", leaf_basis_transfer, leaf_coefficient_rows, precision=exact_product
    )
    coeff_mid = jnp.einsum("ml,ljr->mjr", members, upward_coefficients, precision=exact_product)
    mid_rows = jnp.concatenate([coeff_mid.reshape(mid_count, coeff_width), mid_geom], axis=1)
    top_members = (mid_parent[0][None, :] == jnp.arange(TOP, dtype=jnp.int32)[:, None]).astype(
        jnp.float32
    )
    raised = jnp.einsum("mkj,mkr->mjr", mid_transfer, coeff_mid, precision=exact_product)
    partial_top = jnp.einsum("tm,mjr->tjr", top_members, raised, precision=exact_product)
    coeff_top = lax.psum(partial_top, "leaf")
    top_rows = jnp.concatenate([coeff_top.reshape(TOP, coeff_width), top_geom], axis=1)
    top_all = lax.all_gather(top_rows, "group", axis=0, tiled=True)
    total_tops = top_all.shape[0]
    targets = lax.axis_index("group") * TOP + jnp.arange(TOP, dtype=jnp.int32)
    top_source = (targets[:, None] + top_offsets) % total_tops
    local_top = couple_rows(top_geom, top_all[top_source], table)
    mid_all = lax.all_gather(mid_rows, "leaf", axis=0, tiled=True)
    mid_source = mid_peers * mid_count + mid_slots
    source_point_rows = mid_all[mid_source]
    device_middle_index = jnp.einsum(
        "mkj,mjr->mkr", mid_transfer, local_top[mid_parent[0]], precision=exact_product
    )
    device_middle_index = device_middle_index + couple_rows(mid_geom, source_point_rows, table)
    leaf_index = jnp.arange(leaf_count, dtype=jnp.int32)
    far_ids = leaf_index[:, None] + REACH + leaf_partners[:, NEAR:]
    local_leaf = jnp.einsum(
        "ghw,gwt->ght",
        leaf_basis_transfer,
        device_middle_index[leaf_middle_owner[0]],
        precision=exact_product,
    )
    local_leaf = local_leaf + couple_rows(leaf_geom, leaf_padded[far_ids], table)
    far_product = jnp.einsum("lpk,lkr->rlp", basis, local_leaf, precision=exact_product)
    point_cloud = points.reshape(3, leaf_count, PTS)

    def near_block(block_start):
        block_leaves = block_start * 8 + jnp.arange(8, dtype=jnp.int32)
        offsets = lax.dynamic_slice_in_dim(leaf_partners[:, :NEAR], block_start * 8, 8, 0)
        partner = block_leaves[:, None] + REACH + offsets
        target_cloud = point_cloud[:, block_leaves].transpose(1, 0, 2)
        source = grid[:, partner]
        kernel = matern(target_cloud[:, None], source[RHS:].transpose(1, 2, 0, 3))
        return jnp.einsum("bjpq,rbjq->rbp", kernel, source[:RHS], precision=exact_product)

    near_blocks = lax.map(near_block, jnp.arange(leaf_count // 8, dtype=jnp.int32))
    near_product = near_blocks.transpose(1, 0, 2, 3).reshape(RHS, leaf_count, PTS)
    product = (far_product + near_product) * present[None]
    return product.reshape(RHS, leaf_count * PTS)


def solution(mesh):
    placed = (
        P(None, ("group", "leaf")),
        P(None, ("group", "leaf")),
        P(("group", "leaf")),
        P(("group", "leaf"), None, None),
        P(("group", "leaf"), None),
        P(("group", "leaf"), None),
        P(("group", "leaf"), None),
        P(("group", "leaf"), None, None),
        P(("group", "leaf"), None),
        P("group", "leaf"),
        P(("group", "leaf"), None, None),
        P(("group", "leaf"), None),
        P(("group", "leaf"), None),
        P("group", None),
        P("group", None),
    )
    return jax.shard_map(
        on_device, mesh=mesh, in_specs=placed, out_specs=P(None, ("group", "leaf")), check_vma=False
    )
```

profile of v0, /device:TPU:32, one launch (start us, length us, event | category | flops | bytes accessed | tf_op | source)
XLA Modules:
  0.0 284.0 jit_solution(18294623102038642720)
XLA Ops:
  0.0 0.8 fusion.125
  0.8 0.2 copy-done
  1.0 1.4 fusion.117
  2.4 0.1 copy.61
  2.5 0.2 reshape.349
  2.7 0.8 copy.62
  3.4 3.4 %collective-permute-start = (f32[16,516]{1,0:T(8,128)S(1)}, f32[16,516]{1,0:T(8,128)}, u32[]{:S(2)}, u32[]{:S(2)}) collective-permute-start(f32[16,516]{1,0:T(8,128)S(1)} %pad_maximum_fusion.4), channel_id=1, source_target_pairs={{0,1},{1,2},{2,3},{3,4},{4,5},{5,6},{6,7},{7,8},{8,9},{9,10},{10,1... | collective-permute-start | bytes 99080 | tf_op jit(solution)/shard_map/ppermute | solution.py:22
  6.8 4.6 %collective-permute-start.1 = (f32[16,516]{1,0:T(8,128)S(1)}, f32[16,516]{1,0:T(8,128)}, u32[]{:S(2)}, u32[]{:S(2)}) collective-permute-start(f32[16,516]{1,0:T(8,128)S(1)} %pad_maximum_fusion.4), channel_id=1, source_target_pairs={{1,0},{2,1},{3,2},{4,3},{5,4},{6,5},{7,6},{8,7},{9,8},{10,9},{11,1... | collective-permute-start | bytes 99080 | tf_op jit(solution)/shard_map/ppermute | solution.py:25
  11.4 0.7 lt.115
  12.2 0.9 broadcast_multiply_fusion
  13.1 0.8 pad_maximum_fusion.1
  13.9 1.9 collective-permute-start.2
  15.8 6.0 %collective-permute-start.3 = (f32[19,2048]{1,0:T(8,128)S(1)}, f32[19,2048]{1,0:T(8,128)S(1)}, u32[]{:S(2)}, u32[]{:S(2)}) collective-permute-start(f32[19,2048]{1,0:T(8,128)S(1)} %pad_maximum_fusion.1), channel_id=1, source_target_pairs={{1,0},{2,1},{3,2},{4,3},{5,4},{6,5},{7,6},{8,7},{9,8},{10,9},{11,1... | collective-permute-start | bytes 466952 | tf_op jit(solution)/shard_map/ppermute | solution.py:25
  21.9 1.3 convolution_bitcast_fusion.2
  23.2 0.9 fusion.119
  24.1 0.1 copy.56
  24.2 1.3 convolution_bitcast_fusion.5
  25.5 1.0 fusion.121
  26.5 0.1 copy.51
  26.7 0.2 reshape.345
  26.8 135.6 %psum.7 = f32[16,512]{1,0:T(8,128)S(1)} all-reduce(f32[16,512]{1,0:T(8,128)S(1)} %reshape.345), channel_id=1, replica_groups=mesh['group'=8,'leaf'=32] {'leaf'}, use_global_device_ids=true, to_apply=%region_0.1 | all-reduce | flops 8192 | bytes 65536 | tf_op jit(solution)/shard_map/psum | solution.py:109
  162.4 0.8 copy.52
  163.2 13.4 %all_gather.6 = f32[128,516]{1,0:T(8,128)S(1)} all-gather(f32[16,516]{1,0:T(8,128)S(1)} %pad_maximum_fusion.3), channel_id=1, replica_groups=mesh['group'=8,'leaf'=32] {'group'}, dimensions={0}, use_global_device_ids=true | all-gather | bytes 297216 | tf_op jit(solution)/shard_map/all_gather | solution.py:111
  176.8 1.1 gather_fusion.2
  178.1 0.1 reshape.347
  178.3 54.6 %all_gather.7 = f32[256,516]{1,0:T(8,128)S(1)} all-gather(f32[8,516]{1,0:T(8,128)S(1)} %pad_maximum_fusion.5), channel_id=1, replica_groups=mesh['group'=8,'leaf'=32] {'leaf'}, dimensions={0}, use_global_device_ids=true | all-gather | bytes 544896 | tf_op jit(solution)/shard_map/all_gather | solution.py:116
  233.1 0.7 gather_fusion.4
  233.9 0.2 copy.53
  234.1 0.2 copy.76
  234.3 0.2 multiply_add_fusion
  234.6 0.6 slice_bitcast_fusion.15
  235.2 2.7 reshape.346
  238.0 0.1 copy.58
  238.1 0.1 copy.77
  238.2 0.1 multiply_add_fusion.2
  238.4 0.4 reshape.348
  239.0 0.6 slice_bitcast_fusion.12
  239.6 11.0 %fusion.74 = f32[16,32,16]{1,2,0:T(8,128)S(1)} fusion(f32[16,16,32,16]{3,2,1,0:T(8,128)} %reshape.346, f32[16,16,32]{2,1,0:T(8,128)S(1)} %get-tuple-element.63, f32[16,32]{1,0:T(8,128)} %get-tuple-element.72, f32[16,16,32]{2,1,0:T(8,128)S(1)} %get-tuple-element.64, f32[16,32]{1,0:T(8,128)} %get-tuple-element.73, f32[16,16,32]{2,1,0:T(8,128)S(1)} %get-tuple-element.62, ...), kind=kOutput, calls=%fused_computation.83 | convolution fusion | flops 53477376 | bytes 661504 | tf_op jit(solution)/shard_map/njkm,njmr->nkr/dot_general | solution.py:61
  250.6 0.6 gather_fusion.3
  251.1 2.4 convolution_bitcast_fusion.3
  253.5 0.3 fusion.84
  253.9 0.6 gather_fusion.5
  254.5 0.8 pad_maximum_fusion.2
  255.3 0.8 gather_fusion.6
  256.2 0.2 copy.63
  256.4 0.2 copy.79
  256.5 0.1 multiply_add_fusion.1
  256.7 0.7 slice_bitcast_fusion.6
  257.4 0.7 reshape.350
  258.1 5.7 %fusion.81 = f32[16,32,16]{1,2,0:T(8,128)S(1)} fusion(f32[16,8,32,16]{3,2,1,0:T(8,128)S(1)} %reshape.350, f32[16,8,32]{2,1,0:T(8,128)} %get-tuple-element.66, f32[16,32]{1,0:T(8,128)S(1)} %get-tuple-element.75, f32[16,8,32]{2,1,0:T(8,128)} %get-tuple-element.67, f32[16,32]{1,0:T(8,128)} %get-tuple-element.76, f32[16,8,32]{2,1,0:T(8,128)} %get-tuple-element.65, ...), kind=kOutput, calls=%fused_computation.91 | convolution fusion | flops 26738688 | bytes 350208 | tf_op jit(solution)/shard_map/njkm,njmr->nkr/dot_general | solution.py:61
  263.8 0.5 fusion.80
  264.4 0.1 copy.82
  264.6 0.2 copy.67
  264.7 18.2 %while.10 = (s32[]{:T(128)}, f32[2,16,8,128]{3,1,2,0:T(8,128)S(1)}, s32[2]{0:T(128)S(1)}, s32[16,16]{1,0:T(8,128)S(1)}, f32[19,48,128]{2,0,1:T(8,128)S(1)}, /*in...) while((s32[]{:T(128)}, f32[2,16,8,128]{3,1,2,0:T(8,128)S(1)}, ...), condition=%wide.region_2.3_spmd, body=%wide.region_1.2_spmd.sunk | while | flops 213911856 | bytes 2398031 | solution.py:144
  265.0 0.6 dynamic_slice.11
  266.4 0.6 gather_fusion
  267.2 0.6 gather_fusion.1
  267.8 6.2 %fusion.187 = f32[2,16,8,128]{3,1,2,0:T(8,128)S(1)} fusion(f32[2,16,8,128]{3,1,2,0:T(8,128)S(1)} %get-tuple-element.144, s32[]{:T(128)} %get-tuple-element.143, f32[8,8,128]{2,1,0:T(8,128)S(1)} %bitcast.200, f32[8,128]{1,0:T(8,128)S(1)} %bitcast.208, f32[8,8,128]{2,1,0:T(8,128)S(1)} %bitcast.201, f32[8,128]{1,0:T(8,128)S(1)} %bitcast.209, ...), kind=kOutput, calls=%fused_computation.32.clone.1 | convolution fusion | flops 213909504 | bytes 700420 | tf_op jit(solution)/shard_map/while/body/eval_jaxpr/bjpq,rbjq->rbp/dot_general | solution.py:142
  273.9 0.6 dynamic_slice.11
  275.4 0.6 gather_fusion
  276.2 0.6 gather_fusion.1
  276.8 6.2 %fusion.187 = f32[2,16,8,128]{3,1,2,0:T(8,128)S(1)} fusion(f32[2,16,8,128]{3,1,2,0:T(8,128)S(1)} %get-tuple-element.144, s32[]{:T(128)} %get-tuple-element.143, f32[8,8,128]{2,1,0:T(8,128)S(1)} %bitcast.200, f32[8,128]{1,0:T(8,128)S(1)} %bitcast.208, f32[8,8,128]{2,1,0:T(8,128)S(1)} %bitcast.201, f32[8,128]{1,0:T(8,128)S(1)} %bitcast.209, ...), kind=kOutput, calls=%fused_computation.32.clone.1 | convolution fusion | flops 213909504 | bytes 700420 | tf_op jit(solution)/shard_map/while/body/eval_jaxpr/bjpq,rbjq->rbp/dot_general | solution.py:142
  282.9 0.4 fusion.79
  283.3 0.7 copy.92
  (93 shorter events, 2.0 us)
Async XLA Ops:
  0.0 1.0 copy-start
  0.0 176.6 %copy-start.9 = (s32[16,16]{1,0:T(8,128)S(1)}, s32[16,16]{1,0:T(8,128)}, u32[]{:S(2)}) copy-start(s32[16,16]{1,0:T(8,128)} %param.31) | copy-start | bytes 3076
  3.4 251.0 %collective-permute-start = (f32[16,516]{1,0:T(8,128)S(1)}, f32[16,516]{1,0:T(8,128)}, u32[]{:S(2)}, u32[]{:S(2)}) collective-permute-start(f32[16,516]{1,0:T(8,128)S(1)} %pad_maximum_fusion.4), channel_id=1, source_target_pairs={{0,1},{1,2},{2,3},{3,4},{4,5},{5,6},{6,7},{7,8},{8,9},{9,10},{10,1... | collective-permute-start | bytes 99080 | tf_op jit(solution)/shard_map/ppermute | solution.py:22
  6.8 247.6 %collective-permute-start.1 = (f32[16,516]{1,0:T(8,128)S(1)}, f32[16,516]{1,0:T(8,128)}, u32[]{:S(2)}, u32[]{:S(2)}) collective-permute-start(f32[16,516]{1,0:T(8,128)S(1)} %pad_maximum_fusion.4), channel_id=1, source_target_pairs={{1,0},{2,1},{3,2},{4,3},{5,4},{6,5},{7,6},{8,7},{9,8},{10,9},{11,1... | collective-permute-start | bytes 99080 | tf_op jit(solution)/shard_map/ppermute | solution.py:25
  13.9 250.5 %collective-permute-start.2 = (f32[19,2048]{1,0:T(8,128)S(1)}, f32[19,2048]{1,0:T(8,128)S(1)}, u32[]{:S(2)}, u32[]{:S(2)}) collective-permute-start(f32[19,2048]{1,0:T(8,128)S(1)} %pad_maximum_fusion.1), channel_id=1, source_target_pairs={{0,1},{1,2},{2,3},{3,4},{4,5},{5,6},{6,7},{7,8},{8,9},{9,10},{10,1... | collective-permute-start | bytes 466952 | tf_op jit(solution)/shard_map/ppermute | solution.py:22
  15.8 248.6 %collective-permute-start.3 = (f32[19,2048]{1,0:T(8,128)S(1)}, f32[19,2048]{1,0:T(8,128)S(1)}, u32[]{:S(2)}, u32[]{:S(2)}) collective-permute-start(f32[19,2048]{1,0:T(8,128)S(1)} %pad_maximum_fusion.1), channel_id=1, source_target_pairs={{1,0},{2,1},{3,2},{4,3},{5,4},{6,5},{7,6},{8,7},{9,8},{10,9},{11,1... | collective-permute-start | bytes 466952 | tf_op jit(solution)/shard_map/ppermute | solution.py:25
  24.1 153.9 %copy-start.6 = (f32[16,4]{0,1:T(4,128)S(1)}, f32[16,4]{0,1:T(4,128)}, u32[]{:S(2)}) copy-start(f32[16,4]{0,1:T(4,128)} %param.21) | copy-start | bytes 772
  24.1 153.9 %copy-start.7 = (f32[16,4]{0,1:T(4,128)S(1)}, f32[16,4]{0,1:T(4,128)}, u32[]{:S(2)}) copy-start(f32[16,4]{0,1:T(4,128)} %param.30) | copy-start | bytes 772
  26.6 151.5 %copy-start.12 = (s32[1,8]{1,0:T(1,128)S(1)}, s32[1,8]{1,0:T(1,128)}, u32[]{:S(2)}) copy-start(s32[1,8]{1,0:T(1,128)} %param.26) | copy-start | bytes 100
  26.7 151.6 %copy-start.8 = (f32[8,4]{0,1:T(4,128)S(1)}, f32[8,4]{0,1:T(4,128)}, u32[]{:S(2)}) copy-start(f32[8,4]{0,1:T(4,128)} %param.25) | copy-start | bytes 388
  176.6 56.4 %copy-start.10 = (s32[8,8]{1,0:T(8,128)S(1)}, s32[8,8]{1,0:T(8,128)}, u32[]{:S(2)}) copy-start(s32[8,8]{1,0:T(8,128)} %param.29) | copy-start | bytes 772
  176.6 56.4 %copy-start.11 = (s32[8,8]{1,0:T(8,128)S(1)}, s32[8,8]{1,0:T(8,128)}, u32[]{:S(2)}) copy-start(s32[8,8]{1,0:T(8,128)} %param.28) | copy-start | bytes 772
  176.8 57.1 %copy-start.13 = (s32[1,16]{1,0:T(1,128)S(1)}, s32[1,16]{1,0:T(1,128)}, u32[]{:S(2)}) copy-start(s32[1,16]{1,0:T(1,128)} %param.23) | copy-start | bytes 196
  233.8 5.0 %copy-start.5 = (s32[16,16]{1,0:T(8,128)S(1)}, s32[16,16]{1,0:T(8,128)}, u32[]{:S(2)}) copy-start(s32[16,16]{1,0:T(8,128)} %param.22) | copy-start | bytes 3076
  250.5 3.0 %copy-start.2 = (f32[8,32,32]{2,1,0:T(8,128)S(1)}, f32[8,32,32]{2,1,0:T(8,128)}, u32[]{:S(2)}) copy-start(f32[8,32,32]{2,1,0:T(8,128)} %param.27) | copy-start | bytes 98308
  258.1 5.7 %copy-start.1 = (f32[16,32,32]{2,1,0:T(8,128)S(1)}, f32[16,32,32]{2,1,0:T(8,128)}, u32[]{:S(2)}) copy-start(f32[16,32,32]{2,1,0:T(8,128)} %param.24) | copy-start | bytes 196612
  258.1 6.2 %copy-start.3 = (f32[3,2048]{1,0:T(4,128)S(1)}, f32[3,2048]{1,0:T(4,128)}, u32[]{:S(2)}) copy-start(f32[3,2048]{1,0:T(4,128)} %param.17) | copy-start | bytes 73732
  263.8 1.0 copy-start.4
where the time goes:
time: 285 us; the launch traced here: 284 us
  blocking collectives  204 us (72%)
  matrix products  38.4 us (13%)
  local copies, waits for them, and re-layouts  19.3 us (7%)
  starting transfers between devices  15.9 us (6%)
  other arithmetic  4.5 us (2%)
    psum x1, blocking collectives, on_device(): coeff_top = lax.psum(partial_top, 'leaf')  136 us
    all_gather x1, blocking collectives, on_device(): mid_all = lax.all_gather(mid_rows, 'leaf', axis=0, tiled=True)  54.6 us
    dot_general x3, matrix products, couple_rows(): jnp.einsum('njkm,njmr->nkr', coupling, source_coeff, precision=exact_prod...  19 us
    all_gather x1, blocking collectives, on_device(): top_all = lax.all_gather(top_rows, 'group', axis=0, tiled=True)  13.4 us
    dot_general x2, matrix products, near_block(): jnp.einsum('bjpq,rbjq->rbp', kernel, source[:RHS], precision=exact_product)  12.4 us
    ppermute x2, starting transfers between devices, extended(): lax.ppermute(lax.slice_in_dim(block, 0, width, axis=dim), axis, backward)  10.6 us
  transfers between devices with their start and end apart: 4, of which 0 were waited for; matrix products, arithmetic and copies ran while one was open for 14% of the time, Pallas kernels for 0%

commit v1 on v0

--- a/solution.py
+++ b/solution.py
@@ -106,7 +106,7 @@
     )
     raised = jnp.einsum("mkj,mkr->mjr", mid_transfer, coeff_mid, precision=exact_product)
     partial_top = jnp.einsum("tm,mjr->tjr", top_members, raised, precision=exact_product)
-    coeff_top = lax.psum(partial_top, "leaf")
+    coeff_top = jnp.sum(lax.all_gather(partial_top, "leaf"), axis=0)
     top_rows = jnp.concatenate([coeff_top.reshape(TOP, coeff_width), top_geom], axis=1)
     top_all = lax.all_gather(top_rows, "group", axis=0, tiled=True)
     total_tops = top_all.shape[0]

time: 285 us -> 166 us (0.58)
  blocking collectives: 204 us -> 66.6 us
  between operations: 0.6 us -> 13.9 us
  other arithmetic: 4.5 us -> 8.08 us
    psum x1 -> x0, blocking collectives: 136 us -> none  [on_device(): coeff_top = lax.psum(partial_top, 'leaf')]
  transfers between devices with their start and end apart: 4 -> 5, of which waited for: 0 -> 0; matrix products, arithmetic and copies ran while one was open for 14% -> 25% of each run, Pallas kernels for 0% -> 0%
where the time goes in v1:
time: 166 us; the launch traced here: 165 us
  blocking collectives  66.6 us (40%)
  matrix products  39.5 us (24%)
  local copies, waits for them, and re-layouts  19.3 us (12%)
  starting transfers between devices  15.9 us (10%)
  between operations  13.9 us (8%)
  other arithmetic  8.08 us (5%)
    all_gather x1, blocking collectives, on_device(): mid_all = lax.all_gather(mid_rows, 'leaf', axis=0, tiled=True)  53 us
    dot_general x3, matrix products, couple_rows(): jnp.einsum('njkm,njmr->nkr', coupling, source_coeff, precision=exact_prod...  19.5 us
    all_gather x1, blocking collectives, on_device(): top_all = lax.all_gather(top_rows, 'group', axis=0, tiled=True)  13.5 us
    dot_general x2, matrix products, near_block(): jnp.einsum('bjpq,rbjq->rbp', kernel, source[:RHS], precision=exact_product)  12.4 us
    ppermute x2, starting transfers between devices, extended(): lax.ppermute(lax.slice_in_dim(block, 0, width, axis=dim), axis, backward)  10.6 us
    ppermute x2, starting transfers between devices, extended(): lax.ppermute(lax.slice_in_dim(block, block.shape[dim] - width, None, axis...  5.31 us
    reshape x3, local copies, waits for them, and re-layouts, couple_rows(): source_point_rows[..., :coeff_width]  4.05 us
  transfers between devices with their start and end apart: 5, of which 0 were waited for; matrix products, arithmetic and copies ran while one was open for 25% of the time, Pallas kernels for 0%

profile of v1, /device:TPU:32, one launch (start us, length us, event | category | flops | bytes accessed | tf_op | source)
XLA Modules:
  0.0 165.0 jit_solution(4693450394896980222)
XLA Ops:
  6.6 0.8 fusion.125
  7.5 0.1 copy-done
  7.6 1.4 fusion.117
  9.0 0.1 copy.81
  9.1 0.2 reshape.349
  9.3 0.8 copy.82
  10.1 3.4 %collective-permute-start = (f32[16,516]{1,0:T(8,128)S(1)}, f32[16,516]{1,0:T(8,128)S(1)}, u32[]{:S(2)}, u32[]{:S(2)}) collective-permute-start(f32[16,516]{1,0:T(8,128)S(1)} %pad_maximum_fusion.4), channel_id=1, source_target_pairs={{0,1},{1,2},{2,3},{3,4},{4,5},{5,6},{6,7},{7,8},{8,9},{9,10},{10,1... | collective-permute-start | bytes 99080 | tf_op jit(solution)/shard_map/ppermute | solution.py:22
  13.5 4.6 %collective-permute-start.1 = (f32[16,516]{1,0:T(8,128)S(1)}, f32[16,516]{1,0:T(8,128)S(1)}, u32[]{:S(2)}, u32[]{:S(2)}) collective-permute-start(f32[16,516]{1,0:T(8,128)S(1)} %pad_maximum_fusion.4), channel_id=1, source_target_pairs={{1,0},{2,1},{3,2},{4,3},{5,4},{6,5},{7,6},{8,7},{9,8},{10,9},{11,1... | collective-permute-start | bytes 99080 | tf_op jit(solution)/shard_map/ppermute | solution.py:25
  18.0 0.7 lt.115
  18.8 0.9 broadcast_multiply_fusion
  19.7 0.8 pad_maximum_fusion.1
  20.5 1.9 %collective-permute-start.2 = (f32[19,2048]{1,0:T(8,128)S(1)}, f32[19,2048]{1,0:T(8,128)S(1)}, u32[]{:S(2)}, u32[]{:S(2)}) collective-permute-start(f32[19,2048]{1,0:T(8,128)S(1)} %pad_maximum_fusion.1), channel_id=1, source_target_pairs={{0,1},{1,2},{2,3},{3,4},{4,5},{5,6},{6,7},{7,8},{8,9},{9,10},{10,1... | collective-permute-start | bytes 466952 | tf_op jit(solution)/shard_map/ppermute | solution.py:22
  22.4 6.0 %collective-permute-start.3 = (f32[19,2048]{1,0:T(8,128)S(1)}, f32[19,2048]{1,0:T(8,128)S(1)}, u32[]{:S(2)}, u32[]{:S(2)}) collective-permute-start(f32[19,2048]{1,0:T(8,128)S(1)} %pad_maximum_fusion.1), channel_id=1, source_target_pairs={{1,0},{2,1},{3,2},{4,3},{5,4},{6,5},{7,6},{8,7},{9,8},{10,9},{11,1... | collective-permute-start | bytes 466952 | tf_op jit(solution)/shard_map/ppermute | solution.py:25
  28.4 1.3 convolution_bitcast_fusion.2
  29.7 0.9 fusion.119
  30.7 1.3 convolution_bitcast_fusion.5
  32.0 1.6 fusion.121
  33.8 0.7 slice_bitcast_fusion.19
  34.5 0.7 fusion.148
  35.1 0.1 reshape.347
  35.2 0.8 copy.77
  36.0 53.0 %all_gather.15 = f32[256,516]{1,0:T(8,128)S(1)} all-gather(f32[8,516]{1,0:T(8,128)S(1)} %pad_maximum_fusion.5), channel_id=1, replica_groups=mesh['group'=8,'leaf'=32] {'leaf'}, dimensions={0}, use_global_device_ids=true | all-gather | bytes 544896 | tf_op jit(solution)/shard_map/all_gather | solution.py:116
  89.1 0.7 gather_fusion.4
  90.3 0.6 pad_clamp_fusion.5
  90.9 0.1 copy.78
  91.0 0.1 copy.97
  91.1 0.1 multiply_add_fusion.2
  91.3 0.4 reshape.348
  91.7 0.6 pad_clamp_fusion.3
  92.5 3.0 %convolution_bitcast_fusion.3 = f32[8,32,16]{1,2,0:T(8,128)} fusion(f32[8,8,32,16]{3,2,1,0:T(8,128)S(1)} %reshape.348, f32[8,8,32]{2,1,0:T(8,128)S(1)} %get-tuple-element.75, f32[8,32]{1,0:T(8,128)S(1)} %get-tuple-element.84, f32[8,8,32]{2,1,0:T(8,128)S(1)} %get-tuple-element.76, f32[8,32]{1,0:T(8,128)S(1)} %get-tuple-element.85, ...), kind=kOutput, calls=%fused_computation.92 | convolution fusion | flops 13369344 | bytes 175104 | tf_op jit(solution)/shard_map/njkm,njmr->nkr/dot_general | solution.py:61
  95.6 0.8 gather_fusion.6
  96.6 0.2 copy.83
  96.7 0.2 copy.99
  96.9 0.1 multiply_add_fusion.1
  97.1 0.7 slice_bitcast_fusion.6
  97.8 0.7 reshape.350
  98.5 5.6 %fusion.81 = f32[16,32,16]{1,2,0:T(8,128)S(1)} fusion(f32[16,8,32,16]{3,2,1,0:T(8,128)S(1)} %reshape.350, f32[16,8,32]{2,1,0:T(8,128)} %get-tuple-element.72, f32[16,32]{1,0:T(8,128)S(1)} %get-tuple-element.81, f32[16,8,32]{2,1,0:T(8,128)} %get-tuple-element.73, f32[16,32]{1,0:T(8,128)S(1)} %get-tuple-element.82, f32[16,8,32]{2,1,0:T(8,128)} %get-tuple-element.71, ...), kind=kOutput, calls=%fused_computation.91 | convolution fusion | flops 26738688 | bytes 350208 | tf_op jit(solution)/shard_map/njkm,njmr->nkr/dot_general | solution.py:61
  104.2 0.1 copy.102
  104.3 0.2 copy.87
  104.5 18.3 %while.10 = (s32[]{:T(128)}, f32[2,16,8,128]{3,1,2,0:T(8,128)S(1)}, s32[2]{0:T(128)S(1)}, s32[16,16]{1,0:T(8,128)S(1)}, f32[19,48,128]{2,0,1:T(8,128)S(1)}, /*in...) while((s32[]{:T(128)}, f32[2,16,8,128]{3,1,2,0:T(8,128)S(1)}, ...), condition=%wide.region_2.3_spmd, body=%wide.region_1.2_spmd.sunk | while | flops 213911856 | bytes 2398031 | solution.py:144
  104.7 0.7 dynamic_slice.11
  106.2 0.6 gather_fusion
  107.0 0.6 gather_fusion.1
  107.5 6.2 %fusion.187 = f32[2,16,8,128]{3,1,2,0:T(8,128)S(1)} fusion(f32[2,16,8,128]{3,1,2,0:T(8,128)S(1)} %get-tuple-element.150, s32[]{:T(128)} %get-tuple-element.149, f32[8,8,128]{2,1,0:T(8,128)S(1)} %bitcast.202, f32[8,128]{1,0:T(8,128)S(1)} %bitcast.210, f32[8,8,128]{2,1,0:T(8,128)S(1)} %bitcast.203, f32[8,128]{1,0:T(8,128)S(1)} %bitcast.211, ...), kind=kOutput, calls=%fused_computation.32.clone.1 | convolution fusion | flops 213909504 | bytes 700420 | tf_op jit(solution)/shard_map/while/body/eval_jaxpr/bjpq,rbjq->rbp/dot_general | solution.py:142
  113.7 0.7 dynamic_slice.11
  115.2 0.6 gather_fusion
  116.0 0.6 gather_fusion.1
  116.6 6.2 %fusion.187 = f32[2,16,8,128]{3,1,2,0:T(8,128)S(1)} fusion(f32[2,16,8,128]{3,1,2,0:T(8,128)S(1)} %get-tuple-element.150, s32[]{:T(128)} %get-tuple-element.149, f32[8,8,128]{2,1,0:T(8,128)S(1)} %bitcast.202, f32[8,128]{1,0:T(8,128)S(1)} %bitcast.210, f32[8,8,128]{2,1,0:T(8,128)S(1)} %bitcast.203, f32[8,128]{1,0:T(8,128)S(1)} %bitcast.211, ...), kind=kOutput, calls=%fused_computation.32.clone.1 | convolution fusion | flops 213909504 | bytes 700420 | tf_op jit(solution)/shard_map/while/body/eval_jaxpr/bjpq,rbjq->rbp/dot_general | solution.py:142
  122.8 2.5 %reduce_sum.9 = f32[16,32,16]{1,0,2:T(8,128)S(1)} reduce(f32[32,16,32,16]{2,1,0,3:T(8,128)} %bitcast.190, f32[]{:T(128)} %constant.59.clone.1), dimensions={0}, to_apply=%region_0.1 | reduce | flops 253952 | bytes 1081348 | tf_op jit(solution)/shard_map/reduce_sum | solution.py:109
  125.3 0.1 copy.71
  125.4 0.2 reshape.345
  125.6 13.5 %all_gather.14 = f32[128,516]{1,0:T(8,128)S(1)} all-gather(f32[16,516]{1,0:T(8,128)S(1)} %pad_maximum_fusion.3), channel_id=1, replica_groups=mesh['group'=8,'leaf'=32] {'group'}, dimensions={0}, use_global_device_ids=true | all-gather | bytes 297216 | tf_op jit(solution)/shard_map/all_gather | solution.py:111
  139.1 1.1 gather_fusion.2
  140.4 0.2 copy.73
  140.5 0.2 copy.96
  140.7 0.2 multiply_add_fusion
  141.0 3.0 %reshape.346 = f32[16,16,32,16]{3,2,1,0:T(8,128)} reshape(f32[16,16,512]{2,1,0:T(8,128)S(1)} %slice.202) | data formatting | bytes 1048576 | tf_op jit(solution)/shard_map/reshape | solution.py:57
  144.0 10.9 %fusion.74 = f32[16,32,16]{1,2,0:T(8,128)S(1)} fusion(f32[16,16,32,16]{3,2,1,0:T(8,128)} %reshape.346, f32[16,16,32]{2,1,0:T(8,128)S(1)} %get-tuple-element.69, f32[16,32]{1,0:T(8,128)S(1)} %get-tuple-element.78, f32[16,16,32]{2,1,0:T(8,128)S(1)} %get-tuple-element.70, f32[16,32]{1,0:T(8,128)S(1)} %get-tuple-element.79, ...), kind=kOutput, calls=%fused_computation.83 | convolution fusion | flops 53477376 | bytes 661504 | tf_op jit(solution)/shard_map/njkm,njmr->nkr/dot_general | solution.py:61
  154.8 0.7 gather_fusion.3
  155.6 0.3 fusion.84
  155.9 0.7 gather_fusion.5
  156.6 0.5 fusion.80
  157.1 0.4 fusion.79
  157.5 0.7 copy.112
  (94 shorter events, 2.1 us)
Async XLA Ops:
  6.5 1.0 copy-start
  6.5 83.7 %copy-start.6 = (f32[16,4]{0,1:T(4,128)S(1)}, f32[16,4]{0,1:T(4,128)}, u32[]{:S(2)}) copy-start(f32[16,4]{0,1:T(4,128)} %param.21) | copy-start | bytes 772
  6.5 83.4 %copy-start.12 = (s32[1,16]{1,0:T(1,128)S(1)}, s32[1,16]{1,0:T(1,128)}, u32[]{:S(2)}) copy-start(s32[1,16]{1,0:T(1,128)} %param.23) | copy-start | bytes 196
  6.5 83.4 %copy-start.8 = (f32[8,4]{0,1:T(4,128)S(1)}, f32[8,4]{0,1:T(4,128)}, u32[]{:S(2)}) copy-start(f32[8,4]{0,1:T(4,128)} %param.25) | copy-start | bytes 388
  6.5 82.5 %copy-start.11 = (s32[8,8]{1,0:T(8,128)S(1)}, s32[8,8]{1,0:T(8,128)}, u32[]{:S(2)}) copy-start(s32[8,8]{1,0:T(8,128)} %param.28) | copy-start | bytes 772
  6.5 82.5 %copy-start.10 = (s32[8,8]{1,0:T(8,128)S(1)}, s32[8,8]{1,0:T(8,128)}, u32[]{:S(2)}) copy-start(s32[8,8]{1,0:T(8,128)} %param.29) | copy-start | bytes 772
  6.6 83.4 %copy-start.9 = (s32[16,16]{1,0:T(8,128)S(1)}, s32[16,16]{1,0:T(8,128)}, u32[]{:S(2)}) copy-start(s32[16,16]{1,0:T(8,128)} %param.31) | copy-start | bytes 3076
  6.6 83.6 %copy-start.7 = (f32[16,4]{0,1:T(4,128)S(1)}, f32[16,4]{0,1:T(4,128)}, u32[]{:S(2)}) copy-start(f32[16,4]{0,1:T(4,128)} %param.30) | copy-start | bytes 772
  6.6 85.7 %copy-start.4 = (s32[16,16]{1,0:T(8,128)S(1)}, s32[16,16]{1,0:T(8,128)}, u32[]{:S(2)}) copy-start(s32[16,16]{1,0:T(8,128)} %param.22) | copy-start | bytes 3076
  6.6 116.2 %all-gather.3.cloned.1.call-start = ((), (), s32[]{:S(2)}) async-start(), calls=%async_computation | async-start | bytes 4325376 | tf_op jit(solution)/shard_map/all_gather | solution.py:109
  10.1 85.5 %collective-permute-start = (f32[16,516]{1,0:T(8,128)S(1)}, f32[16,516]{1,0:T(8,128)S(1)}, u32[]{:S(2)}, u32[]{:S(2)}) collective-permute-start(f32[16,516]{1,0:T(8,128)S(1)} %pad_maximum_fusion.4), channel_id=1, source_target_pairs={{0,1},{1,2},{2,3},{3,4},{4,5},{5,6},{6,7},{7,8},{8,9},{9,10},{10,1... | collective-permute-start | bytes 99080 | tf_op jit(solution)/shard_map/ppermute | solution.py:22
  13.5 82.2 %collective-permute-start.1 = (f32[16,516]{1,0:T(8,128)S(1)}, f32[16,516]{1,0:T(8,128)S(1)}, u32[]{:S(2)}, u32[]{:S(2)}) collective-permute-start(f32[16,516]{1,0:T(8,128)S(1)} %pad_maximum_fusion.4), channel_id=1, source_target_pairs={{1,0},{2,1},{3,2},{4,3},{5,4},{6,5},{7,6},{8,7},{9,8},{10,9},{11,1... | collective-permute-start | bytes 99080 | tf_op jit(solution)/shard_map/ppermute | solution.py:25
  20.5 83.6 %collective-permute-start.2 = (f32[19,2048]{1,0:T(8,128)S(1)}, f32[19,2048]{1,0:T(8,128)S(1)}, u32[]{:S(2)}, u32[]{:S(2)}) collective-permute-start(f32[19,2048]{1,0:T(8,128)S(1)} %pad_maximum_fusion.1), channel_id=1, source_target_pairs={{0,1},{1,2},{2,3},{3,4},{4,5},{5,6},{6,7},{7,8},{8,9},{9,10},{10,1... | collective-permute-start | bytes 466952 | tf_op jit(solution)/shard_map/ppermute | solution.py:22
  22.4 81.7 %collective-permute-start.3 = (f32[19,2048]{1,0:T(8,128)S(1)}, f32[19,2048]{1,0:T(8,128)S(1)}, u32[]{:S(2)}, u32[]{:S(2)}) collective-permute-start(f32[19,2048]{1,0:T(8,128)S(1)} %pad_maximum_fusion.1), channel_id=1, source_target_pairs={{1,0},{2,1},{3,2},{4,3},{5,4},{6,5},{7,6},{8,7},{9,8},{10,9},{11,1... | collective-permute-start | bytes 466952 | tf_op jit(solution)/shard_map/ppermute | solution.py:25
  98.5 5.7 %copy-start.3 = (f32[3,2048]{1,0:T(4,128)S(1)}, f32[3,2048]{1,0:T(4,128)}, u32[]{:S(2)}) copy-start(f32[3,2048]{1,0:T(4,128)} %param.17) | copy-start | bytes 73732
  144.0 11.6 %copy-start.2 = (f32[8,32,32]{2,1,0:T(8,128)S(1)}, f32[8,32,32]{2,1,0:T(8,128)}, u32[]{:S(2)}) copy-start(f32[8,32,32]{2,1,0:T(8,128)} %param.27) | copy-start | bytes 98308
  144.0 11.6 %copy-start.5 = (f32[8,32,16]{1,2,0:T(8,128)S(1)}, f32[8,32,16]{1,2,0:T(8,128)}, u32[]{:S(2)}) copy-start(f32[8,32,16]{1,2,0:T(8,128)} %convolution_bitcast_fusion.3) | copy-start | bytes 49156
  144.0 12.6 %copy-start.1 = (f32[16,32,32]{2,1,0:T(8,128)S(1)}, f32[16,32,32]{2,1,0:T(8,128)}, u32[]{:S(2)}) copy-start(f32[16,32,32]{2,1,0:T(8,128)} %param.24) | copy-start | bytes 196612
Sparse Core Ops, SparseCore 0:
  33.8 87.0 all-gather.2
